TPU v7x, 32 devices: a whole 2x2x4 slice. The times are simulated.
32 devices in a mesh: gx: 4 (over y, x), gy: 8 (over z, core).
Axes of the slice: x: 2, y: 2, z: 4, core: 2. Of those that a mesh axis runs over, the one named last changes fastest.
Arguments:
- inputs: bfloat16 [16, 16, 32, 512], P('gx', 'gy'), may hold values from -6 to 6
- cotangent: bfloat16 [16, 16, 32, 512], P('gx', 'gy'), may hold values from -6 to 6
- point_weight: bfloat16 [32, 32], replicated, may hold values from -1 to 1
- spectral_weight: bfloat16 [2304, 24, 2048], P(('gx', 'gy')), may hold values from -0.75 to 0.75
Outputs:
- grad_input: bfloat16 [16, 16, 32, 512], P('gx', 'gy')
- grad_spectral: float32 [2304, 24, 2048], P(('gx', 'gy'))
All inputs are finite; a program needn't handle non-finite values.
Results may differ from a plain program's by a relative error of at most 0.034.
Values may be sent and summed in bfloat16 or wider, within the bound.
No kernel may reach another device: no remote copies, remote signals or barrier semaphores. Data moves between devices by JAX's collectives and lax.ppermute only.
A program may use at most 192 MiB of HBM per device.

v0:
```python
import math
import jax
import jax.numpy as jnp
from jax import lax
from jax.sharding import PartitionSpec as P

NZ = 64
NT = 8
KX = 24
KY = 24
KZ = 12
KT = 8


def kept_angles(positions, kept_count, length):
    index = jnp.arange(kept_count, dtype=jnp.int32)
    frequency = jnp.where(index < kept_count // 2, index, index - kept_count)
    turns = positions[:, None] * frequency[None, :] % length
    return turns.astype(jnp.float32) * (2.0 * math.pi / length)


def axis_tables(positions, kept_count, length):
    angles = kept_angles(positions, kept_count, length)
    return (jnp.cos(angles), jnp.sin(angles))


def depth_tables():
    angle_depth = kept_angles(jnp.arange(NZ, dtype=jnp.int32), KZ, NZ)
    angle_time = kept_angles(jnp.arange(NT, dtype=jnp.int32), KT, NT)
    angles = (angle_depth[:, None, :, None] + angle_time[None, :, None, :]).reshape(
        NZ * NT, KZ * KT
    )
    return (jnp.cos(angles), jnp.sin(angles))


def settle(values):
    return lax.optimization_barrier(values.astype(jnp.bfloat16))


def rotate(spectra, cosine_table, sine_table, pattern, turn_sign):
    half_width = spectra.shape[-1] // 2
    with_cosine = jnp.einsum(pattern, spectra, cosine_table, precision=lax.Precision.HIGHEST)
    with_sine = jnp.einsum(pattern, spectra, sine_table, precision=lax.Precision.HIGHEST)
    real_part = with_cosine[..., :half_width] + turn_sign * with_sine[..., half_width:]
    imag_part = with_cosine[..., half_width:] - turn_sign * with_sine[..., :half_width]
    return jnp.concatenate([real_part, imag_part], -1)


def depth_forward(field_in, tables, factor):
    widened = field_in.astype(jnp.float32)
    with_cosine = jnp.einsum("xycs,sk->kxyc", widened, tables[0], precision=lax.Precision.HIGHEST)
    with_sine = jnp.einsum("xycs,sk->kxyc", widened, tables[1], precision=lax.Precision.HIGHEST)
    return jnp.concatenate([with_cosine, -with_sine], -1) * factor


def depth_inverse(spectra, tables, factor):
    half_width = spectra.shape[-1] // 2
    with_cosine = jnp.einsum(
        "kxyc,sk->xycs", spectra[..., :half_width], tables[0], precision=lax.Precision.HIGHEST
    )
    with_sine = jnp.einsum(
        "kxyc,sk->xycs", spectra[..., half_width:], tables[1], precision=lax.Precision.HIGHEST
    )
    return (with_cosine - with_sine) * factor


def contract_in(left, right):
    return jnp.einsum("mkc,mkco->mko", left, right, precision=lax.Precision.HIGHEST)


def contract_out(left, right):
    return jnp.einsum("mko,mkco->mkc", left, right, precision=lax.Precision.HIGHEST)


def partial_outer(left, right):
    return jnp.einsum("mkc,mko->mkco", left, right, precision=lax.Precision.HIGHEST)


def mix_modes(spectra, weight):
    half_width = spectra.shape[-1] // 2
    weight_wide = weight.astype(jnp.float32)
    weight_real, weight_imag = (weight_wide[..., :half_width], weight_wide[..., half_width:])
    real_in, imag_in = (spectra[..., :half_width], spectra[..., half_width:])
    real_out = contract_in(real_in, weight_real) - contract_in(imag_in, weight_imag)
    imag_out = contract_in(real_in, weight_imag) + contract_in(imag_in, weight_real)
    return jnp.concatenate([real_out, imag_out], -1)


def adjoint_modes(spectra, weight):
    half_width = spectra.shape[-1] // 2
    weight_wide = weight.astype(jnp.float32)
    weight_real, weight_imag = (weight_wide[..., :half_width], weight_wide[..., half_width:])
    real_in, imag_in = (spectra[..., :half_width], spectra[..., half_width:])
    real_out = contract_out(real_in, weight_real) + contract_out(imag_in, weight_imag)
    imag_out = contract_out(imag_in, weight_real) - contract_out(real_in, weight_imag)
    return jnp.concatenate([real_out, imag_out], -1)


def weight_grad(spectra_in, spectra_back):
    half_width = spectra_in.shape[-1] // 2
    real_in, imag_in = (spectra_in[..., :half_width], spectra_in[..., half_width:])
    real_back, imag_back = (spectra_back[..., :half_width], spectra_back[..., half_width:])
    real_part = partial_outer(real_in, real_back) + partial_outer(imag_in, imag_back)
    imag_part = partial_outer(real_in, imag_back) - partial_outer(imag_in, real_back)
    return jnp.concatenate([real_part, imag_part], -1)


def exact_gelu(values):
    return jax.nn.gelu(values, approximate=False)


def per_device(inputs, cotangent, point_weight, spectral_weight):
    rows_x, rows_y, channels, cells = inputs.shape
    mode_rows, mode_cols, flat_width = spectral_weight.shape
    weight_blocks = spectral_weight.reshape(mode_rows, mode_cols, channels, 2 * channels)
    count_gx = lax.axis_size("gx")
    count_gy = lax.axis_size("gy")
    length_x = rows_x * count_gx
    length_y = rows_y * count_gy
    depth_pair = depth_tables()
    own_x = lax.axis_index("gx") * rows_x + jnp.arange(rows_x, dtype=jnp.int32)
    local_x = axis_tables(own_x, KX, length_x)
    whole_y = axis_tables(jnp.arange(length_y, dtype=jnp.int32), KY, length_y)
    total_cells = length_x * length_y * cells
    kept_total = KX * KY * KZ * KT

    def to_modes(field_in, factor):
        depth_spec = settle(depth_forward(field_in, depth_pair, factor))
        share = depth_spec.shape[0] // count_gx
        first_spectra = lax.psum_scatter(
            rotate(
                depth_spec.astype(jnp.float32), local_x[0], local_x[1], "rxyc,xk->rkyc", 1.0
            ).astype(jnp.bfloat16),
            "gx",
            scatter_dimension=0,
            tiled=True,
        ).astype(jnp.float32)
        first_spectra = settle(first_spectra).reshape(share * KX, rows_y, 2 * channels)
        arrived_modes = lax.all_to_all(first_spectra, "gy", split_axis=0, concat_axis=1, tiled=True)
        return rotate(arrived_modes.astype(jnp.float32), whole_y[0], whole_y[1], "myc,yk->mkc", 1.0)

    def to_space(spectra, factor):
        back_rows = settle(rotate(spectra, whole_y[0], whole_y[1], "mkc,yk->myc", -1.0))
        returned = lax.all_to_all(back_rows, "gy", split_axis=1, concat_axis=0, tiled=True)
        share = returned.shape[0] // KX
        returned = returned.reshape(share, KX, rows_y, 2 * channels)
        back_depth = settle(
            rotate(
                lax.all_gather(returned, "gx", axis=0, tiled=True).astype(jnp.float32),
                local_x[0],
                local_x[1],
                "rkyc,xk->rxyc",
                -1.0,
            )
        )
        return depth_inverse(back_depth.astype(jnp.float32), depth_pair, factor)

    spectra_in = to_modes(inputs, 1.0 / math.sqrt(total_cells))
    mixed = mix_modes(spectra_in, weight_blocks)
    spectral_out = to_space(mixed, 1.0 / math.sqrt(kept_total))
    pointwise = jnp.einsum(
        "xycs,co->xyos", inputs, point_weight, preferred_element_type=jnp.float32
    )
    before = spectral_out + pointwise
    unused_out, pullback = jax.vjp(exact_gelu, before)
    slope = settle(pullback(cotangent.astype(jnp.float32))[0])
    spectra_back = to_modes(slope, 1.0 / math.sqrt(kept_total))
    grad_spectral = weight_grad(spectra_in, spectra_back).reshape(mode_rows, mode_cols, flat_width)
    adjoint = adjoint_modes(spectra_back, weight_blocks)
    spectral_grad = to_space(adjoint, 1.0 / math.sqrt(total_cells))
    pointwise_grad = jnp.einsum(
        "xyos,co->xycs", slope, point_weight, preferred_element_type=jnp.float32
    )
    grad_input = (pointwise_grad + spectral_grad).astype(jnp.bfloat16)
    return (grad_input, grad_spectral)


def solution(mesh):
    placed = (
        P("gx", "gy", None, None),
        P("gx", "gy", None, None),
        P(),
        P(("gx", "gy"), None, None),
    )
    return jax.shard_map(
        per_device,
        mesh=mesh,
        in_specs=placed,
        out_specs=(P("gx", "gy", None, None), P(("gx", "gy"), None, None)),
        check_vma=False,
    )
```

profile of v0, /device:TPU:0, one launch (start us, length us, event | category | flops | bytes accessed | tf_op | source)
XLA Modules:
  0.0 453.6 jit_solution(6818993007358127799)
XLA Ops:
  7.4 12.3 %add_sine_fusion = (f32[64,8,12,8]{1,0,3,2:T(8,128)}, f32[64,8,12,8]{1,0,3,2:T(8,128)S(1)}) fusion(f32[8,8]{0,1:T(8,128)S(1)} %fusion.94, f32[64,12]{0,1:T(8,128)S(1)} %fusion.75), kind=kLoop, calls=%fused_computation.19 | loop fusion | flops 49152 | bytes 396544 | tf_op jit(solution)/shard_map/sin | solution.py:33
  19.8 3.9 reshape.129
  23.7 2.8 reshape.128
  26.5 1.3 convolution_negate_fusion.1
  27.8 1.3 fusion.52
  29.1 1.0 convolution_bitcast_fusion.2
  30.1 1.0 convolution_bitcast_fusion.3
  31.4 1.6 copy.73
  33.1 31.4 %reduce-scatter.3.cloned.1.call-done = bf16[24,24,2,64]{3,1,2,0:T(8,128)(2,1)} async-done(((bf16[96,24,2,64]{3,1,2,0:T(8,128)(2,1)}), bf16[24,24,2,64]{3,1,2,0:T(8,128)(2,1)}) %reduce-scatter.3.cloned.1.call-update) | async-done | bytes 147472 | tf_op jit(solution)/shard_map/reduce_scatter | solution.py:130
  64.5 1.0 copy.74
  65.8 0.9 reshape.154
  66.7 4.6 %all-to-all-start = ((bf16[8,2,4608]{2,1,0:T(2,128)(2,1)}), bf16[8,2,4608]{2,1,0:T(2,128)(2,1)S(1)}, u32[]{:S(2)}, u32[]{:S(2)}) async-start(bf16[8,2,4608]{2,1,0:T(2,128)(2,1)} %reshape.154), calls=%async_computation.1 | async-start | bytes 294912 | tf_op jit(solution)/shard_map/all_to_all | solution.py:139
  71.3 0.6 reduce-scatter.5.cloned.1.call-start
  71.8 20.8 %reshape.123 = bf16[72,24,32,64]{3,2,1,0:T(8,128)(2,1)} reshape(bf16[72,24,2048]{2,1,0:T(8,128)(2,1)} %param.7) | data formatting | bytes 14155776 | tf_op jit(solution)/shard_map/reshape | solution.py:115
  93.4 0.6 convolution_bitcast_fusion.6
  94.0 0.6 convolution_bitcast_fusion.7
  95.3 34.3 %fusion.2 = (f32[72,24,32]{2,1,0:T(8,128)}, f32[72,24,32]{2,1,0:T(8,128)}, f32[72,24,32]{2,1,0:T(8,128)}, f32[72,24,32]{2,1,0:T(8,128)S(1)}) fusion(f32[72,24,32]{2,1,0:T(8,128)S(1)} %copy.146, bf16[72,24,32,64]{3,2,1,0:T(8,128)(2,1)} %reshape.123, f32[72,24,32]{2,1,0:T(8,128)S(1)} %copy.145), kind=kLoop, calls=%fused_computation.10 | loop fusion | flops 17473536 | bytes 8404992
  129.7 2.3 copy.111
  131.9 2.2 copy.119
  134.1 2.2 copy.115
  136.3 1.0 copy.107
  137.3 1.2 add.210
  138.5 1.2 sub.98
  139.7 0.6 convolution_bitcast_fusion.12
  140.3 0.6 convolution_bitcast_fusion.13
  141.1 14.6 %all_to_all.66 = bf16[72,16,64]{0,2,1:T(8,128)(2,1)S(1)} all-to-all(bf16[72,16,64]{0,2,1:T(8,128)(2,1)S(1)} %copy.78), channel_id=1, replica_groups=mesh['gx'=4,'gy'=8] {'gy'}, dimensions={1} | all-to-all | bytes 294912 | tf_op jit(solution)/shard_map/all_to_all | solution.py:144
  155.7 0.9 copy.79
  156.6 1.4 copy.80
  158.0 38.1 %all_gather.6 = bf16[96,24,2,64]{1,0,3,2:T(8,128)(2,1)S(1)} all-gather(bf16[24,24,2,64]{1,0,3,2:T(8,128)(2,1)S(1)} %copy.80), channel_id=1, replica_groups=mesh['gx'=4,'gy'=8] {'gx'}, dimensions={0}, use_global_device_ids=true | all-gather | bytes 737280 | tf_op jit(solution)/shard_map/all_gather | solution.py:149
  196.1 5.8 %convolution_bitcast_fusion.16 = f32[96,4,2,64]{0,1,3,2:T(4,128)S(1)} fusion(bf16[96,24,2,64]{1,0,3,2:T(8,128)(2,1)S(1)} %all_gather.6, s32[24]{0:T(128)S(1)} %compare_select_fusion.2, s32[4]{0:T(128)S(1)} %iota_add_fusion), kind=kOutput, calls=%fused_computation.44 | convolution fusion | flops 14157120 | bytes 786544 | tf_op jit(solution)/shard_map/rkyc,xk->rxyc/dot_general | solution.py:43
  201.9 5.8 %convolution_bitcast_fusion.17 = f32[96,4,2,64]{0,1,3,2:T(4,128)S(1)} fusion(bf16[96,24,2,64]{1,0,3,2:T(8,128)(2,1)S(1)} %all_gather.6, s32[24]{0:T(128)S(1)} %compare_select_fusion.2, s32[4]{0:T(128)S(1)} %iota_add_fusion), kind=kOutput, calls=%fused_computation.45 | convolution fusion | flops 14157120 | bytes 786544 | tf_op jit(solution)/shard_map/rkyc,xk->rxyc/dot_general | solution.py:42
  208.1 0.4 fusion.50
  208.5 0.4 fusion.10
  208.9 2.4 fusion.22
  212.1 1.0 convolution_bitcast_fusion
  213.1 1.0 convolution_bitcast_fusion.1
  214.4 1.7 copy.86
  216.1 27.9 %reduce-scatter.5.cloned.1.call-done = bf16[24,24,2,64]{3,1,2,0:T(8,128)(2,1)} async-done(((bf16[96,24,2,64]{3,1,2,0:T(8,128)(2,1)}), bf16[24,24,2,64]{3,1,2,0:T(8,128)(2,1)}) %reduce-scatter.5.cloned.1.call-update) | async-done | bytes 147472 | tf_op jit(solution)/shard_map/reduce_scatter | solution.py:130
  244.0 1.0 copy.87
  245.5 11.6 %all_to_all.67 = bf16[8,2,4608]{2,1,0:T(2,128)(2,1)S(1)} all-to-all(bf16[8,2,4608]{2,1,0:T(2,128)(2,1)S(1)} %reshape.156), channel_id=1, replica_groups=mesh['gx'=4,'gy'=8] {'gy'}, dimensions={0} | all-to-all | bytes 294912 | tf_op jit(solution)/shard_map/all_to_all | solution.py:139
  257.8 0.6 convolution_bitcast_fusion.4
  258.4 0.6 convolution_bitcast_fusion.5
  259.0 1.0 slice_add_fusion.2
  259.9 1.3 copy.147
  261.3 2.3 copy.148
  263.6 38.7 %fusion.6 = (f32[72,24,32]{2,1,0:T(8,128)}, f32[72,24,32]{2,1,0:T(8,128)}, f32[72,24,32]{2,1,0:T(8,128)}, f32[72,24,32]{2,1,0:T(8,128)}) fusion(f32[72,24,32]{2,1,0:T(8,128)} %copy.148, bf16[72,24,32,64]{3,2,1,0:T(8,128)(2,1)} %reshape.123, f32[72,24,32]{2,1,0:T(8,128)S(1)} %copy.147), kind=kLoop, calls=%fused_computation.14 | loop fusion | flops 17473536 | bytes 8404992
  302.3 2.2 copy.131
  304.4 2.2 copy.136
  306.6 2.2 copy.141
  308.8 2.2 copy.126
  311.0 1.2 sub.104
  312.2 1.2 add.216
  313.4 0.6 convolution_bitcast_fusion.9
  314.0 0.6 convolution_bitcast_fusion.10
  314.6 20.0 %multiply_add_fusion = (f32[72,24,32,32]{3,2,1,0:T(8,128)}, f32[72,24,32,32]{3,2,1,0:T(8,128)}) fusion(f32[72,24,32]{2,1,0:T(8,128)S(1)} %copy.146, f32[72,24,32]{2,1,0:T(8,128)S(1)} %copy.145, f32[72,24,32]{2,1,0:T(8,128)} %copy.148, f32[72,24,32]{2,1,0:T(8,128)S(1)} %copy.147), kind=kLoop, calls=%fused_computation.18 | loop fusion | flops 10616832 | bytes 15040512 | tf_op jit(solution)/shard_map/add | solution.py:103
  334.7 0.8 copy.91
  335.5 3.7 all-to-all-start.3
  339.2 28.5 %pad_maximum_fusion = f32[72,24,32,64]{3,2,1,0:T(8,128)} fusion(f32[72,24,32,32]{3,2,1,0:T(8,128)} %get-tuple-element.15, f32[72,24,32,32]{3,2,1,0:T(8,128)} %get-tuple-element.14), kind=kLoop, calls=%fused_computation.16 | loop fusion | flops 3538944 | bytes 28311552 | tf_op jit(solution)/shard_map/concatenate | solution.py:105
  367.7 24.3 %reshape.127 = f32[72,24,2048]{2,1,0:T(8,128)} reshape(f32[72,24,32,64]{3,2,1,0:T(8,128)} %pad_maximum_fusion) | data formatting | bytes 28311552 | tf_op jit(solution)/shard_map/reshape | solution.py:168
  392.2 0.4 copy.93
  392.7 40.0 %all_gather.7 = bf16[96,24,2,64]{1,0,3,2:T(8,128)(2,1)S(1)} all-gather(bf16[24,24,2,64]{1,0,3,2:T(8,128)(2,1)S(1)} %copy.93), channel_id=1, replica_groups=mesh['gx'=4,'gy'=8] {'gx'}, dimensions={0}, use_global_device_ids=true | all-gather | bytes 737280 | tf_op jit(solution)/shard_map/all_gather | solution.py:149
  432.7 5.8 %convolution_bitcast_fusion.14 = f32[96,4,2,64]{0,1,3,2:T(4,128)S(1)} fusion(bf16[96,24,2,64]{1,0,3,2:T(8,128)(2,1)S(1)} %all_gather.7, s32[24]{0:T(128)S(1)} %compare_select_fusion.2, s32[4]{0:T(128)S(1)} %iota_add_fusion), kind=kOutput, calls=%fused_computation.42 | convolution fusion | flops 14157120 | bytes 786544 | tf_op jit(solution)/shard_map/rkyc,xk->rxyc/dot_general | solution.py:43
  438.5 5.8 %convolution_bitcast_fusion.15 = f32[96,4,2,64]{0,1,3,2:T(4,128)S(1)} fusion(bf16[96,24,2,64]{1,0,3,2:T(8,128)(2,1)S(1)} %all_gather.7, s32[24]{0:T(128)S(1)} %compare_select_fusion.2, s32[4]{0:T(128)S(1)} %iota_add_fusion), kind=kOutput, calls=%fused_computation.43 | convolution fusion | flops 14157120 | bytes 786544 | tf_op jit(solution)/shard_map/rkyc,xk->rxyc/dot_general | solution.py:42
  445.4 0.9 fusion.12
  (59 shorter events, 6.6 us)
Async XLA Ops:
  7.2 19.3 %copy-start = (bf16[4,2,32,512]{3,2,1,0:T(8,128)(2,1)S(1)}, bf16[4,2,32,512]{3,2,1,0:T(8,128)(2,1)}, u32[]{:S(2)}) copy-start(bf16[4,2,32,512]{3,2,1,0:T(8,128)(2,1)} %param.4) | copy-start | bytes 786436
  7.2 57.3 %reduce-scatter.3.cloned.1.call-start = ((), (), s32[]{:S(2)}) async-start(), calls=%async_computation.6 | async-start | bytes 1474560 | tf_op jit(solution)/shard_map/reduce_scatter | solution.py:130
  66.7 26.0 %all-to-all-start = ((bf16[8,2,4608]{2,1,0:T(2,128)(2,1)}), bf16[8,2,4608]{2,1,0:T(2,128)(2,1)S(1)}, u32[]{:S(2)}, u32[]{:S(2)}) async-start(bf16[8,2,4608]{2,1,0:T(2,128)(2,1)} %reshape.154), calls=%async_computation.1 | async-start | bytes 294912 | tf_op jit(solution)/shard_map/all_to_all | solution.py:139
  71.3 172.7 %reduce-scatter.5.cloned.1.call-start = ((), (), s32[]{:S(2)}) async-start(), calls=%async_computation.7 | async-start | bytes 1474560 | tf_op jit(solution)/shard_map/reduce_scatter | solution.py:130
  129.6 78.4 %copy-start.3 = (f32[512,96,1,1]{0,1,2,3:T(8,128)S(1)}, f32[512,96,1,1]{0,1,2,3:T(8,128)}, u32[]{:S(2)}) copy-start(f32[512,96,1,1]{0,1,2,3:T(8,128)} %reshape.128) | copy-start | bytes 589828
  129.7 78.8 %copy-start.2 = (f32[512,96,1,1]{0,1,2,3:T(8,128)S(1)}, f32[512,96,1,1]{0,1,2,3:T(8,128)}, u32[]{:S(2)}) copy-start(f32[512,96,1,1]{0,1,2,3:T(8,128)} %reshape.129) | copy-start | bytes 589828
  129.7 79.2 %copy-start.6 = (bf16[32,32]{1,0:T(8,128)(2,1)S(1)}, bf16[32,32]{1,0:T(8,128)(2,1)}, u32[]{:S(2)}) copy-start(bf16[32,32]{1,0:T(8,128)(2,1)} %param.6) | copy-start | bytes 6148
  211.2 3.0 copy-start.4
  335.5 56.5 %all-to-all-start.3 = ((bf16[72,16,64]{0,2,1:T(8,128)(2,1)}), bf16[72,16,64]{0,2,1:T(8,128)(2,1)S(1)}, u32[]{:S(2)}, u32[]{:S(2)}) async-start(bf16[72,16,64]{0,2,1:T(8,128)(2,1)} %copy.91), calls=%async_computation.5 | async-start | bytes 524288 | tf_op jit(solution)/shard_map/all_to_all | solution.py:144
  367.7 78.6 %copy-start.1 = (bf16[4,2,32,512]{3,2,1,0:T(8,128)(2,1)S(1)}, bf16[4,2,32,512]{3,2,1,0:T(8,128)(2,1)}, u32[]{:S(2)}) copy-start(bf16[4,2,32,512]{3,2,1,0:T(8,128)(2,1)} %param.4) | copy-start | bytes 786436
  392.0 53.4 %copy-start.5 = (bf16[4,2,32,512]{3,2,1,0:T(8,128)(2,1)S(1)}, bf16[4,2,32,512]{3,2,1,0:T(8,128)(2,1)}, u32[]{:S(2)}) copy-start(bf16[4,2,32,512]{3,2,1,0:T(8,128)(2,1)} %copy-done.4) | copy-start | bytes 786436
Sparse Core Ops, SparseCore 0:
  33.2 31.2 reduce-scatter.2
  216.2 27.7 reduce-scatter.4
where the time goes:
time: 463 us; the launch traced here: 454 us
  other arithmetic  141 us (30%)
  blocking collectives  104 us (22%)
  local copies, waits for them, and re-layouts  84.9 us (18%)
  waiting for transfers between devices  59.4 us (13%)
  matrix products  40.2 us (9%)
  between operations  15 us (3%)
  starting transfers between devices  8.86 us (2%)
    all_gather x2, blocking collectives, to_space(): lax.all_gather(returned, 'gx', axis=0, tiled=True).astype(jnp.float32)  78.1 us
    unnamed x2, other arithmetic  73 us
    reduce_scatter x2, waiting for transfers between devices, to_modes(): lax.psum_scatter(rotate(depth_spec.astype(jnp.float32), local_x[0], local...  59.3 us
    concatenate x1, other arithmetic, weight_grad(): return jnp.concatenate([real_part, imag_part], -1)  28.5 us
    reshape x1, local copies, waits for them, and re-layouts, per_device(): weight_grad(spectra_in, spectra_back)  24.3 us
    reshape x1, local copies, waits for them, and re-layouts, per_device(): spectral_weight.reshape(mode_rows, mode_cols, channels, 2 * channels)  20.8 us
    add x1, other arithmetic, weight_grad(): partial_outer(real_in, real_back) + partial_outer(imag_in, imag_back)  20 us
    dot_general x8, matrix products, rotate(): jnp.einsum(pattern, spectra, cosine_table, precision=lax.Precision.HIGHEST)  16 us
  transfers between devices with their start and end apart: 4, of which 2 were waited for; matrix products, arithmetic and copies ran while one was open for 16% of the time, Pallas kernels for 0%

commit v1 on v0

--- a/solution.py
+++ b/solution.py
@@ -141,7 +141,12 @@
 
     def to_space(spectra, factor):
         back_rows = settle(rotate(spectra, whole_y[0], whole_y[1], "mkc,yk->myc", -1.0))
-        returned = lax.all_to_all(back_rows, "gy", split_axis=1, concat_axis=0, tiled=True)
+        returned = jnp.concatenate(
+            lax.all_to_all(
+                jnp.stack(jnp.split(back_rows, lax.axis_size("gy"), axis=1)), "gy", 0, 0
+            ),
+            axis=0,
+        )
         share = returned.shape[0] // KX
         returned = returned.reshape(share, KX, rows_y, 2 * channels)
         back_depth = settle(

time: 463 us -> 467 us (level)
  local copies, waits for them, and re-layouts: 84.9 us -> 89.6 us
    unnamed x22 -> x36, local copies, waits for them, and re-layouts: 5.86 us -> 10.7 us
where the time goes in v1:
time: 467 us; the launch traced here: 458 us
  other arithmetic  141 us (30%)
  blocking collectives  104 us (22%)
  local copies, waits for them, and re-layouts  89.6 us (19%)
  waiting for transfers between devices  59.4 us (13%)
  matrix products  40.2 us (9%)
  between operations  15 us (3%)
  starting transfers between devices  8.86 us (2%)
    all_gather x2, blocking collectives, to_space(): lax.all_gather(returned, 'gx', axis=0, tiled=True).astype(jnp.float32)  78.1 us
    unnamed x2, other arithmetic  73 us
    reduce_scatter x2, waiting for transfers between devices, to_modes(): lax.psum_scatter(rotate(depth_spec.astype(jnp.float32), local_x[0], local...  59.3 us
    concatenate x1, other arithmetic, weight_grad(): return jnp.concatenate([real_part, imag_part], -1)  28.5 us
    reshape x1, local copies, waits for them, and re-layouts, per_device(): weight_grad(spectra_in, spectra_back)  24.3 us
    reshape x1, local copies, waits for them, and re-layouts, per_device(): spectral_weight.reshape(mode_rows, mode_cols, channels, 2 * channels)  20.8 us
    add x1, other arithmetic, weight_grad(): partial_outer(real_in, real_back) + partial_outer(imag_in, imag_back)  20 us
    dot_general x8, matrix products, rotate(): jnp.einsum(pattern, spectra, cosine_table, precision=lax.Precision.HIGHEST)  16 us
  transfers between devices with their start and end apart: 4, of which 2 were waited for; matrix products, arithmetic and copies ran while one was open for 16% of the time, Pallas kernels for 0%

profile of v1, /device:TPU:0, one launch (start us, length us, event | category | flops | bytes accessed | tf_op | source)
XLA Modules:
  0.0 458.3 jit_solution(5512247143777212666)
XLA Ops:
  7.4 12.3 %add_sine_fusion = (f32[64,8,12,8]{1,0,3,2:T(8,128)}, f32[64,8,12,8]{1,0,3,2:T(8,128)S(1)}) fusion(f32[8,8]{0,1:T(8,128)S(1)} %fusion.94, f32[64,12]{0,1:T(8,128)S(1)} %fusion.75), kind=kLoop, calls=%fused_computation.19 | loop fusion | flops 49152 | bytes 396544 | tf_op jit(solution)/shard_map/sin | solution.py:33
  19.8 3.9 reshape.119
  23.7 2.8 reshape.118
  26.5 1.3 convolution_negate_fusion.1
  27.8 1.3 fusion.52
  29.1 1.0 convolution_bitcast_fusion.2
  30.1 1.0 convolution_bitcast_fusion.3
  31.4 1.6 copy.44
  33.1 31.4 %reduce-scatter.3.cloned.1.call-done = bf16[24,24,2,64]{3,1,2,0:T(8,128)(2,1)} async-done(((bf16[96,24,2,64]{3,1,2,0:T(8,128)(2,1)}), bf16[24,24,2,64]{3,1,2,0:T(8,128)(2,1)}) %reduce-scatter.3.cloned.1.call-update) | async-done | bytes 147472 | tf_op jit(solution)/shard_map/reduce_scatter | solution.py:130
  64.5 1.0 copy.45
  65.8 0.9 reshape.144
  66.7 4.6 %all-to-all-start = ((bf16[8,2,4608]{2,1,0:T(2,128)(2,1)}), bf16[8,2,4608]{2,1,0:T(2,128)(2,1)S(1)}, u32[]{:S(2)}, u32[]{:S(2)}) async-start(bf16[8,2,4608]{2,1,0:T(2,128)(2,1)} %reshape.144), calls=%async_computation.1 | async-start | bytes 294912 | tf_op jit(solution)/shard_map/all_to_all | solution.py:139
  71.8 20.8 %reshape.115 = bf16[72,24,32,64]{3,2,1,0:T(8,128)(2,1)} reshape(bf16[72,24,2048]{2,1,0:T(8,128)(2,1)} %param.7) | data formatting | bytes 14155776 | tf_op jit(solution)/shard_map/reshape | solution.py:115
  93.4 0.6 convolution_bitcast_fusion.6
  95.3 34.3 %fusion.2 = (f32[72,24,32]{2,1,0:T(8,128)}, f32[72,24,32]{2,1,0:T(8,128)}, f32[72,24,32]{2,1,0:T(8,128)}, f32[72,24,32]{2,1,0:T(8,128)S(1)}) fusion(f32[72,24,32]{2,1,0:T(8,128)S(1)} %copy.115, bf16[72,24,32,64]{3,2,1,0:T(8,128)(2,1)} %reshape.115, f32[72,24,32]{2,1,0:T(8,128)S(1)} %copy.114), kind=kLoop, calls=%fused_computation.10 | loop fusion | flops 17473536 | bytes 8404992
  129.7 2.3 copy.80
  131.9 2.2 copy.88
  134.1 2.2 copy.84
  136.3 1.0 copy.76
  137.3 1.2 add.210
  138.5 1.2 sub.98
  139.7 0.6 convolution_bitcast_fusion.12
  140.3 0.6 convolution_bitcast_fusion.13
  141.5 14.6 %all_to_all.46 = bf16[8,72,2,64]{1,2,3,0:T(2,128)(2,1)S(1)} all-to-all(bf16[8,72,2,64]{1,2,3,0:T(2,128)(2,1)S(1)} %constant_dynamic-update-slice_fusion), channel_id=1, replica_groups=mesh['gx'=4,'gy'=8] {'gy'}, dimensions={0} | all-to-all | bytes 294912 | tf_op jit(solution)/shard_map/all_to_all | solution.py:145
  156.1 0.9 copy.49
  156.9 1.4 copy.50
  158.3 38.1 %all_gather.6 = bf16[96,24,2,64]{1,0,3,2:T(8,128)(2,1)S(1)} all-gather(bf16[24,24,2,64]{1,0,3,2:T(8,128)(2,1)S(1)} %copy.50), channel_id=1, replica_groups=mesh['gx'=4,'gy'=8] {'gx'}, dimensions={0}, use_global_device_ids=true | all-gather | bytes 737280 | tf_op jit(solution)/shard_map/all_gather | solution.py:154
  196.4 5.8 %convolution_bitcast_fusion.16 = f32[96,4,2,64]{0,1,3,2:T(4,128)S(1)} fusion(bf16[96,24,2,64]{1,0,3,2:T(8,128)(2,1)S(1)} %all_gather.6, s32[24]{0:T(128)S(1)} %compare_select_fusion.2, s32[4]{0:T(128)S(1)} %iota_add_fusion), kind=kOutput, calls=%fused_computation.44 | convolution fusion | flops 14157120 | bytes 786544 | tf_op jit(solution)/shard_map/rkyc,xk->rxyc/dot_general | solution.py:43
  202.2 5.8 %convolution_bitcast_fusion.17 = f32[96,4,2,64]{0,1,3,2:T(4,128)S(1)} fusion(bf16[96,24,2,64]{1,0,3,2:T(8,128)(2,1)S(1)} %all_gather.6, s32[24]{0:T(128)S(1)} %compare_select_fusion.2, s32[4]{0:T(128)S(1)} %iota_add_fusion), kind=kOutput, calls=%fused_computation.45 | convolution fusion | flops 14157120 | bytes 786544 | tf_op jit(solution)/shard_map/rkyc,xk->rxyc/dot_general | solution.py:42
  209.2 2.4 fusion.22
  212.4 1.0 convolution_bitcast_fusion
  213.4 1.0 convolution_bitcast_fusion.1
  214.7 1.7 copy.56
  216.4 27.9 %reduce-scatter.5.cloned.1.call-done = bf16[24,24,2,64]{3,1,2,0:T(8,128)(2,1)} async-done(((bf16[96,24,2,64]{3,1,2,0:T(8,128)(2,1)}), bf16[24,24,2,64]{3,1,2,0:T(8,128)(2,1)}) %reduce-scatter.5.cloned.1.call-update) | async-done | bytes 147472 | tf_op jit(solution)/shard_map/reduce_scatter | solution.py:130
  244.3 1.0 copy.57
  245.8 11.6 %all_to_all.47 = bf16[8,2,4608]{2,1,0:T(2,128)(2,1)S(1)} all-to-all(bf16[8,2,4608]{2,1,0:T(2,128)(2,1)S(1)} %reshape.146), channel_id=1, replica_groups=mesh['gx'=4,'gy'=8] {'gy'}, dimensions={0} | all-to-all | bytes 294912 | tf_op jit(solution)/shard_map/all_to_all | solution.py:139
  259.3 1.0 slice_add_fusion.2
  260.3 1.3 copy.116
  261.6 2.3 copy.117
  263.9 38.7 %fusion.6 = (f32[72,24,32]{2,1,0:T(8,128)}, f32[72,24,32]{2,1,0:T(8,128)}, f32[72,24,32]{2,1,0:T(8,128)}, f32[72,24,32]{2,1,0:T(8,128)}) fusion(f32[72,24,32]{2,1,0:T(8,128)} %copy.117, bf16[72,24,32,64]{3,2,1,0:T(8,128)(2,1)} %reshape.115, f32[72,24,32]{2,1,0:T(8,128)S(1)} %copy.116), kind=kLoop, calls=%fused_computation.14 | loop fusion | flops 17473536 | bytes 8404992
  302.6 2.2 copy.100
  304.8 2.2 copy.105
  307.0 2.2 copy.110
  309.2 2.2 copy.95
  311.4 1.2 sub.104
  312.5 1.2 add.216
  313.7 0.6 convolution_bitcast_fusion.9
  314.3 0.6 convolution_bitcast_fusion.10
  314.9 20.0 %multiply_add_fusion = (f32[72,24,32,32]{3,2,1,0:T(8,128)}, f32[72,24,32,32]{3,2,1,0:T(8,128)}) fusion(f32[72,24,32]{2,1,0:T(8,128)S(1)} %copy.115, f32[72,24,32]{2,1,0:T(8,128)S(1)} %copy.114, f32[72,24,32]{2,1,0:T(8,128)} %copy.117, f32[72,24,32]{2,1,0:T(8,128)S(1)} %copy.116), kind=kLoop, calls=%fused_computation.18 | loop fusion | flops 10616832 | bytes 15040512 | tf_op jit(solution)/shard_map/add | solution.py:103
  335.1 0.6 constant_dynamic-update-slice_fusion.15
  335.7 0.7 constant_dynamic-update-slice_fusion.14
  336.3 0.7 constant_dynamic-update-slice_fusion.13
  337.0 0.7 constant_dynamic-update-slice_fusion.12
  337.6 0.6 constant_dynamic-update-slice_fusion.11
  338.3 0.7 constant_dynamic-update-slice_fusion.10
  338.9 0.7 constant_dynamic-update-slice_fusion.9
  339.6 0.7 constant_dynamic-update-slice_fusion.8
  340.2 3.7 all-to-all-start.3
  343.9 28.5 %pad_maximum_fusion = f32[72,24,32,64]{3,2,1,0:T(8,128)} fusion(f32[72,24,32,32]{3,2,1,0:T(8,128)} %get-tuple-element.15, f32[72,24,32,32]{3,2,1,0:T(8,128)} %get-tuple-element.14), kind=kLoop, calls=%fused_computation.16 | loop fusion | flops 3538944 | bytes 28311552 | tf_op jit(solution)/shard_map/concatenate | solution.py:105
  372.4 24.3 %reshape.117 = f32[72,24,2048]{2,1,0:T(8,128)} reshape(f32[72,24,32,64]{3,2,1,0:T(8,128)} %pad_maximum_fusion) | data formatting | bytes 28311552 | tf_op jit(solution)/shard_map/reshape | solution.py:173
  397.4 40.0 %all_gather.7 = bf16[96,24,2,64]{1,0,3,2:T(8,128)(2,1)S(1)} all-gather(bf16[24,24,2,64]{1,0,3,2:T(8,128)(2,1)S(1)} %copy.62), channel_id=1, replica_groups=mesh['gx'=4,'gy'=8] {'gx'}, dimensions={0}, use_global_device_ids=true | all-gather | bytes 737280 | tf_op jit(solution)/shard_map/all_gather | solution.py:154
  437.4 5.8 %convolution_bitcast_fusion.14 = f32[96,4,2,64]{0,1,3,2:T(4,128)S(1)} fusion(bf16[96,24,2,64]{1,0,3,2:T(8,128)(2,1)S(1)} %all_gather.7, s32[24]{0:T(128)S(1)} %compare_select_fusion.2, s32[4]{0:T(128)S(1)} %iota_add_fusion), kind=kOutput, calls=%fused_computation.42 | convolution fusion | flops 14157120 | bytes 786544 | tf_op jit(solution)/shard_map/rkyc,xk->rxyc/dot_general | solution.py:43
  443.2 5.8 %convolution_bitcast_fusion.15 = f32[96,4,2,64]{0,1,3,2:T(4,128)S(1)} fusion(bf16[96,24,2,64]{1,0,3,2:T(8,128)(2,1)S(1)} %all_gather.7, s32[24]{0:T(128)S(1)} %compare_select_fusion.2, s32[4]{0:T(128)S(1)} %iota_add_fusion), kind=kOutput, calls=%fused_computation.43 | convolution fusion | flops 14157120 | bytes 786544 | tf_op jit(solution)/shard_map/rkyc,xk->rxyc/dot_general | solution.py:42
  450.1 0.9 fusion.12
  (73 shorter events, 10.4 us)
Async XLA Ops:
  7.2 19.3 %copy-start = (bf16[4,2,32,512]{3,2,1,0:T(8,128)(2,1)S(1)}, bf16[4,2,32,512]{3,2,1,0:T(8,128)(2,1)}, u32[]{:S(2)}) copy-start(bf16[4,2,32,512]{3,2,1,0:T(8,128)(2,1)} %param.4) | copy-start | bytes 786436
  7.2 57.3 %reduce-scatter.3.cloned.1.call-start = ((), (), s32[]{:S(2)}) async-start(), calls=%async_computation.6 | async-start | bytes 1474560 | tf_op jit(solution)/shard_map/reduce_scatter | solution.py:130
  66.7 26.0 %all-to-all-start = ((bf16[8,2,4608]{2,1,0:T(2,128)(2,1)}), bf16[8,2,4608]{2,1,0:T(2,128)(2,1)S(1)}, u32[]{:S(2)}, u32[]{:S(2)}) async-start(bf16[8,2,4608]{2,1,0:T(2,128)(2,1)} %reshape.144), calls=%async_computation.1 | async-start | bytes 294912 | tf_op jit(solution)/shard_map/all_to_all | solution.py:139
  71.3 173.1 %reduce-scatter.5.cloned.1.call-start = ((), (), s32[]{:S(2)}) async-start(), calls=%async_computation.7 | async-start | bytes 1474560 | tf_op jit(solution)/shard_map/reduce_scatter | solution.py:130
  129.6 78.7 %copy-start.3 = (f32[512,96,1,1]{0,1,2,3:T(8,128)S(1)}, f32[512,96,1,1]{0,1,2,3:T(8,128)}, u32[]{:S(2)}) copy-start(f32[512,96,1,1]{0,1,2,3:T(8,128)} %reshape.118) | copy-start | bytes 589828
  129.7 79.1 %copy-start.2 = (f32[512,96,1,1]{0,1,2,3:T(8,128)S(1)}, f32[512,96,1,1]{0,1,2,3:T(8,128)}, u32[]{:S(2)}) copy-start(f32[512,96,1,1]{0,1,2,3:T(8,128)} %reshape.119) | copy-start | bytes 589828
  129.7 79.5 %copy-start.6 = (bf16[32,32]{1,0:T(8,128)(2,1)S(1)}, bf16[32,32]{1,0:T(8,128)(2,1)}, u32[]{:S(2)}) copy-start(bf16[32,32]{1,0:T(8,128)(2,1)} %param.6) | copy-start | bytes 6148
  211.6 3.0 copy-start.4
  340.2 56.5 %all-to-all-start.3 = ((bf16[8,72,2,64]{1,2,3,0:T(2,128)(2,1)}), bf16[8,72,2,64]{1,2,3,0:T(2,128)(2,1)S(1)}, u32[]{:S(2)}, u32[]{:S(2)}) async-start(bf16[8,72,2,64]{1,2,3,0:T(2,128)(2,1)} %constant_dynamic-update-slice_fusion.8), calls=%async_computation.5 | async-start | bytes 524288 | tf_op jit(solution)/shard_map/all_to_all | solution.py:145
  372.4 78.6 %copy-start.1 = (bf16[4,2,32,512]{3,2,1,0:T(8,128)(2,1)S(1)}, bf16[4,2,32,512]{3,2,1,0:T(8,128)(2,1)}, u32[]{:S(2)}) copy-start(bf16[4,2,32,512]{3,2,1,0:T(8,128)(2,1)} %param.4) | copy-start | bytes 786436
  396.8 53.4 %copy-start.5 = (bf16[4,2,32,512]{3,2,1,0:T(8,128)(2,1)S(1)}, bf16[4,2,32,512]{3,2,1,0:T(8,128)(2,1)}, u32[]{:S(2)}) copy-start(bf16[4,2,32,512]{3,2,1,0:T(8,128)(2,1)} %copy-done.4) | copy-start | bytes 786436
Sparse Core Ops, SparseCore 0:
  33.2 31.2 reduce-scatter.2
  216.5 27.7 reduce-scatter.4
